TPU v7x, 32 devices: a whole 2x2x4 slice. The times are simulated.
32 devices in a mesh: dp: 2 (over x), row: 4 (over y, core), col: 4 (over z).
Axes of the slice: x: 2, y: 2, z: 4, core: 2. Of those that a mesh axis runs over, the one named last changes fastest.
Arguments:
- tokens: bfloat16 [768, 39200], P('row', ('dp', 'col')), may hold values from -6 to 6
- grad_out: bfloat16 [768, 39200], P('row', ('dp', 'col')), may hold values from -6 to 6
- adapter_index: int32 [8, 1], replicated, may hold values from 0 to 7
- norm1_gain: bfloat16 [768], P('row'), may hold values from 0.099609375 to 1.8984375
- norm2_gain: bfloat16 [768], P('row'), may hold values from 0.099609375 to 1.8984375
- qkv_weight: bfloat16 [768, 2304], P('row', 'col'), may hold values from -0.21875 to 0.21875
- proj_weight: bfloat16 [768, 768], P('col', 'row'), may hold values from -0.875 to 0.875
- fc1_weight: bfloat16 [768, 3072], P('row', 'col'), may hold values from -0.21875 to 0.21875
- fc2_weight: bfloat16 [768, 3072], P('row', 'col'), may hold values from -0.109375 to 0.109375
- rel_h: bfloat16 [27, 64], replicated, may hold values from -0.59765625 to 0.59765625
- rel_w: bfloat16 [27, 64], replicated, may hold values from -0.59765625 to 0.59765625
- qkv_down: bfloat16 [8, 768, 16], P(None, 'row'), may hold values from -0.21875 to 0.21875
- qkv_up: bfloat16 [8, 16, 2304], P(None, None, 'col'), may hold values from -0.75 to 0.75
- proj_down: bfloat16 [8, 768, 16], P(None, 'col'), may hold values from -0.21875 to 0.21875
- proj_up: bfloat16 [8, 16, 768], P(None, None, 'row'), may hold values from -0.75 to 0.75
- fc1_down: bfloat16 [8, 768, 16], P(None, 'row'), may hold values from -0.21875 to 0.21875
- fc1_up: bfloat16 [8, 16, 3072], P(None, None, 'col'), may hold values from -0.75 to 0.75
- fc2_down: bfloat16 [8, 3072, 16], P(None, 'col'), may hold values from -0.109375 to 0.109375
- fc2_up: bfloat16 [8, 16, 768], P(None, None, 'row'), may hold values from -0.75 to 0.75
Outputs:
- out: bfloat16 [768, 39200], P('row', ('dp', 'col'))
- tokens_grad: float32 [768, 39200], P('row', ('dp', 'col'))
- qkv_down_grad: float32 [8, 768, 16], P(None, 'row')
- qkv_up_grad: float32 [8, 16, 2304], P(None, None, 'col')
- proj_down_grad: float32 [8, 768, 16], P(None, 'col')
- proj_up_grad: float32 [8, 16, 768], P(None, None, 'row')
- fc1_down_grad: float32 [8, 768, 16], P(None, 'row')
- fc1_up_grad: float32 [8, 16, 3072], P(None, None, 'col')
- fc2_down_grad: float32 [8, 3072, 16], P(None, 'col')
- fc2_up_grad: float32 [8, 16, 768], P(None, None, 'row')
Inputs may be any that keep to these rules, and one draw needn't show every extreme that they name: `adapter_index`: every one of the 8 adapters is chosen by at least one image.
All inputs are finite; a program needn't handle non-finite values.
Results may differ from a plain program's by a relative error of at most 0.015.
Values may be sent and summed in bfloat16 or wider, within the bound.
No kernel may reach another device: no remote copies, remote signals or barrier semaphores. Data moves between devices by JAX's collectives and lax.ppermute only.
A program may use at most 448 MiB of HBM per device.

v0:
```python
import jax
import jax.numpy as jnp
from jax import lax
from jax.sharding import PartitionSpec as P

D = 768
HD = 64
WIN = 14
SIDE = 64
ADAPT = 8
NWIN_SIDE = 5
IMG_TOK = 4900
PRECISE = lax.Precision.HIGHEST
EPSILON = 1e-06


def exact_gelu(values):
    return jax.nn.gelu(values, approximate=False)


def valid_rows():
    position = jnp.arange(IMG_TOK, dtype=jnp.int32)
    window = position // (WIN * WIN)
    inside = position % (WIN * WIN)
    image_row = window // NWIN_SIDE * WIN + inside // WIN
    image_col = window % NWIN_SIDE * WIN + inside % WIN
    return ((image_row < SIDE) & (image_col < SIDE)).astype(jnp.float32)


def rel_table(rel_param):
    offsets = (
        jnp.arange(WIN, dtype=jnp.int32)[:, None]
        - jnp.arange(WIN, dtype=jnp.int32)[None, :]
        + WIN
        - 1
    )
    one_hot = (
        offsets[:, :, None] == jnp.arange(2 * WIN - 1, dtype=jnp.int32)[None, None, :]
    ).astype(jnp.bfloat16)
    return jnp.einsum("akn,nc->akc", one_hot, rel_param, preferred_element_type=jnp.float32).astype(
        jnp.bfloat16
    )


def pick_one(adapter, own_pick):
    return jnp.einsum("a,ade->de", own_pick, adapter.astype(jnp.float32), precision=PRECISE).astype(
        jnp.bfloat16
    )


def row_totals(first_sum, second_sum):
    return lax.psum((first_sum, second_sum), "row")


def norm_forward(values):
    totals = row_totals(jnp.sum(values, axis=1), jnp.sum(values * values, axis=1))
    center = totals[0] / D
    inv_std = lax.rsqrt(totals[1] / D - center * center + EPSILON)
    return ((values - center[:, None]) * inv_std[:, None], inv_std)


def norm_backward(grad_normed, normed, inv_std):
    totals = row_totals(jnp.sum(grad_normed, axis=1), jnp.sum(grad_normed * normed, axis=1))
    return inv_std[:, None] * (
        grad_normed - totals[0][:, None] / D - normed * totals[1][:, None] / D
    )


def local_norm(values):
    center = jnp.sum(values, axis=1) / D
    inv_std = lax.rsqrt(jnp.sum(values * values, axis=1) / D - center * center + EPSILON)
    return ((values - center[:, None]) * inv_std[:, None], inv_std)


def local_norm_back(grad_normed, normed, inv_std):
    first_mean = jnp.sum(grad_normed, axis=1) / D
    second_mean = jnp.sum(grad_normed * normed, axis=1) / D
    return inv_std[:, None] * (grad_normed - first_mean[:, None] - normed * second_mean[:, None])


def to_features(values):
    return lax.all_to_all(
        values.astype(jnp.bfloat16), "row", split_axis=0, concat_axis=1, tiled=True
    ).astype(values.dtype)


def to_tokens(values):
    return lax.all_to_all(
        values.astype(jnp.bfloat16), "row", split_axis=1, concat_axis=0, tiled=True
    ).astype(values.dtype)


def token_rows(values):
    return lax.all_to_all(values, "row", split_axis=0, concat_axis=1, tiled=True)


def head_cols(values):
    return lax.all_to_all(values, "row", split_axis=1, concat_axis=0, tiled=True)


def head_sums(values):
    return lax.all_to_all(
        values.astype(jnp.bfloat16), "row", split_axis=1, concat_axis=0, tiled=True
    ).astype(values.dtype)


def adapted_local(inputs, weight, down_mat, up_mat):
    product = jnp.dot(inputs, weight, preferred_element_type=jnp.float32)
    reduced = jnp.dot(inputs, down_mat, preferred_element_type=jnp.float32)
    return product + jnp.dot(reduced, up_mat.astype(jnp.float32), precision=PRECISE)


def adapted_back(grads, weight, down_mat, up_mat):
    contract = (((1,), (1,)), ((), ()))
    product = lax.dot_general(grads, weight, contract, preferred_element_type=jnp.float32)
    reduced = lax.dot_general(grads, up_mat, contract, preferred_element_type=jnp.float32)
    return product + lax.dot_general(
        reduced, down_mat.astype(jnp.float32), contract, precision=PRECISE
    )


def pair_grads(inputs_m, grads_m, down_m, up_m):
    reduced = jnp.dot(inputs_m, down_m, preferred_element_type=jnp.float32)
    back_red = lax.dot_general(
        grads_m, up_m, (((1,), (1,)), ((), ())), preferred_element_type=jnp.float32
    )
    grad_down = jnp.einsum("td,tr->dr", inputs_m, back_red, precision=PRECISE)
    grad_up = jnp.einsum("tr,to->ro", reduced, grads_m, precision=PRECISE)
    return (grad_down, grad_up)


def spread_pick(own_pick, grad_mat):
    return jnp.einsum("a,de->ade", own_pick, grad_mat)


def take_block(full, dim, index, length):
    return lax.dynamic_slice_in_dim(full, index * length, length, dim)


def split_qkv(qkv_low):
    heads_local = qkv_low.shape[1] // (3 * HD)
    arranged = qkv_low.reshape(NWIN_SIDE * NWIN_SIDE, WIN * WIN, heads_local, 3, HD)
    return (arranged[:, :, :, 0], arranged[:, :, :, 1], arranged[:, :, :, 2])


def score_matrix(query_b, key_b, tables):
    windows = query_b.shape[0]
    heads_local = query_b.shape[2]
    dot_scores = jnp.einsum(
        "nqhc,nkhc->nhqk", query_b, key_b, preferred_element_type=jnp.float32
    ) * HD ** (-0.5)
    spatial = query_b.reshape(windows, WIN, WIN, heads_local, HD)
    rel_rows = jnp.einsum(
        "nabhc,akc->nhabk", spatial, tables[0], preferred_element_type=jnp.float32
    )
    rel_cols = jnp.einsum(
        "nabhc,bkc->nhabk", spatial, tables[1], preferred_element_type=jnp.float32
    )
    shaped = dot_scores.reshape(windows, heads_local, WIN, WIN, WIN, WIN)
    shaped = shaped + rel_rows[:, :, :, :, :, None] + rel_cols[:, :, :, :, None, :]
    return shaped.reshape(windows, heads_local, WIN * WIN, WIN * WIN)


def attend(qkv_low, tables):
    query_b, key_b, value_b = split_qkv(qkv_low)
    scores = score_matrix(query_b, key_b, tables)
    maxima = jnp.max(scores, axis=3, keepdims=True)
    exponent = jnp.exp(scores - maxima)
    sum_exp = jnp.sum(exponent, axis=3, keepdims=True)
    attn_prob = (exponent / sum_exp).astype(jnp.bfloat16)
    attended = jnp.einsum("nhqk,nkhc->nqhc", attn_prob, value_b, preferred_element_type=jnp.float32)
    log_total = (maxima + jnp.log(sum_exp))[:, :, :, 0]
    return (attended.reshape(IMG_TOK, attended.shape[2] * HD).astype(jnp.bfloat16), log_total)


def attend_back(qkv_low, log_total, grad_attended, tables):
    query_b, key_b, value_b = split_qkv(qkv_low)
    windows = query_b.shape[0]
    heads_local = query_b.shape[2]
    scores = score_matrix(query_b, key_b, tables)
    attn_exact = jnp.exp(scores - log_total[:, :, :, None])
    prob_low = attn_exact.astype(jnp.bfloat16)
    grad_o = grad_attended.reshape(windows, WIN * WIN, heads_local, HD)
    grad_v = jnp.einsum("nhqk,nqhc->nkhc", prob_low, grad_o, preferred_element_type=jnp.float32)
    grad_p = jnp.einsum("nqhc,nkhc->nhqk", grad_o, value_b, preferred_element_type=jnp.float32)
    centre = jnp.sum(grad_p * attn_exact, axis=3, keepdims=True)
    grad_s = (attn_exact * (grad_p - centre)).astype(jnp.bfloat16)
    grad_q = jnp.einsum(
        "nhqk,nkhc->nqhc", grad_s, key_b, preferred_element_type=jnp.float32
    ) * HD ** (-0.5)
    grad_k = jnp.einsum(
        "nhqk,nqhc->nkhc", grad_s, query_b, preferred_element_type=jnp.float32
    ) * HD ** (-0.5)
    split_grad = grad_s.astype(jnp.float32).reshape(windows, heads_local, WIN, WIN, WIN, WIN)
    along_rows = jnp.sum(split_grad, axis=5)
    along_cols = jnp.sum(split_grad, axis=4)
    rel_grad = jnp.einsum(
        "nhabk,akc->nabhc", along_rows, tables[0].astype(jnp.float32), precision=PRECISE
    )
    rel_grad = rel_grad + jnp.einsum(
        "nhabk,bkc->nabhc", along_cols, tables[1].astype(jnp.float32), precision=PRECISE
    )
    grad_q = grad_q + rel_grad.reshape(windows, WIN * WIN, heads_local, HD)
    stacked = jnp.stack([grad_q, grad_k, grad_v], axis=3)
    return stacked.reshape(IMG_TOK, heads_local * 3 * HD).astype(jnp.bfloat16)


def body(
    tokens,
    grad_out,
    adapter_index,
    norm1_gain,
    norm2_gain,
    qkv_weight,
    proj_weight,
    fc1_weight,
    fc2_weight,
    rel_h,
    rel_w,
    qkv_down,
    qkv_up,
    proj_down,
    proj_up,
    fc1_down,
    fc1_up,
    fc2_down,
    fc2_up,
):
    members = lax.axis_size("col")
    row_index = lax.axis_index("row")
    col_index = lax.axis_index("col")
    group_ids = lax.dynamic_slice_in_dim(
        adapter_index[:, 0], lax.axis_index("dp") * members, members, 0
    )
    chosen = (group_ids[:, None] == jnp.arange(ADAPT, dtype=jnp.int32)[None, :]).astype(jnp.float32)
    own_pick = chosen[col_index]
    validity = valid_rows()[:, None]
    tables = (rel_table(rel_h), rel_table(rel_w))
    inputs = tokens.astype(jnp.float32).T
    normed_one, inv_one = norm_forward(inputs)
    gain_one = norm1_gain.astype(jnp.float32)
    hidden_one = (normed_one * gain_one * validity).astype(jnp.bfloat16)
    qkv_part, proj_part, qkv_dn_part, proj_up_part = (
        lax.all_gather(qkv_weight, "row", axis=0, tiled=True),
        lax.all_gather(proj_weight, "row", axis=1, tiled=True),
        lax.all_gather(qkv_down, "row", axis=1, tiled=True),
        lax.all_gather(proj_up, "row", axis=2, tiled=True),
    )
    qkv_full, proj_full, qkv_up_all, proj_dn_all = (
        lax.all_gather(qkv_part, "col", axis=1, tiled=True),
        lax.all_gather(proj_part, "col", axis=0, tiled=True),
        lax.all_gather(qkv_up, "col", axis=2, tiled=True),
        lax.all_gather(proj_down, "col", axis=1, tiled=True),
    )
    qkv_dn = pick_one(qkv_dn_part, own_pick)
    qkv_upm = pick_one(qkv_up_all, own_pick)
    proj_dn = pick_one(proj_dn_all, own_pick)
    proj_upm = pick_one(proj_up_part, own_pick)
    hidden_rows = token_rows(hidden_one)
    qkv_rows_out = adapted_local(hidden_rows, qkv_full, qkv_dn, qkv_upm).astype(jnp.bfloat16)
    qkv_low = head_cols(qkv_rows_out)
    attended, log_total = attend(qkv_low, tables)
    attended_rows = token_rows(attended)
    branch = head_sums(adapted_local(attended_rows, proj_full, proj_dn, proj_upm))
    middle = inputs + branch
    grad_final = grad_out.astype(jnp.float32).T * validity
    weight_up, weight_stored, down_one, up_two, gain_full = (
        lax.all_gather(fc1_weight, "row", axis=0, tiled=True),
        lax.all_gather(fc2_weight, "row", axis=0, tiled=True),
        lax.all_gather(fc1_down, "row", axis=1, tiled=True),
        lax.all_gather(fc2_up, "row", axis=2, tiled=True),
        lax.all_gather(norm2_gain, "row", axis=0, tiled=True),
    )
    weight_up, weight_stored, up_one, down_two = (
        lax.all_gather(weight_up, "col", axis=1, tiled=True),
        lax.all_gather(weight_stored, "col", axis=1, tiled=True),
        lax.all_gather(fc1_up, "col", axis=2, tiled=True),
        lax.all_gather(fc2_down, "col", axis=1, tiled=True),
    )
    weight_down = weight_stored.T
    down_fc1 = pick_one(down_one, own_pick)
    up_fc1 = pick_one(up_one, own_pick)
    down_fc2 = pick_one(down_two, own_pick)
    up_fc2 = pick_one(up_two, own_pick)
    local_mid = to_features(middle)
    normed_two, inv_two = local_norm(local_mid)
    gain_two = gain_full.astype(jnp.float32)
    hidden_two = (normed_two * gain_two).astype(jnp.bfloat16)
    pre_act = adapted_local(hidden_two, weight_up, down_fc1, up_fc1)
    activated = exact_gelu(pre_act).astype(jnp.bfloat16)
    mlp_out = to_tokens(adapted_local(activated, weight_down, down_fc2, up_fc2))
    grad_local = to_features(grad_final).astype(jnp.bfloat16)
    grad_activ = adapted_back(grad_local, weight_down, down_fc2, up_fc2)
    gelu_value, gelu_back = jax.vjp(exact_gelu, pre_act)
    grad_pre = gelu_back(grad_activ)[0].astype(jnp.bfloat16)
    grad_hidden_two = adapted_back(grad_pre, weight_up, down_fc1, up_fc1)
    grad_middle = grad_final + to_tokens(
        local_norm_back(grad_hidden_two * gain_two, normed_two, inv_two)
    )
    fc1_local = pair_grads(hidden_two, grad_pre, down_fc1, up_fc1)
    fc2_local = pair_grads(activated, grad_local, down_fc2, up_fc2)
    summed_all = lax.psum(
        (
            spread_pick(own_pick, fc1_local[0]),
            spread_pick(own_pick, fc1_local[1]),
            spread_pick(own_pick, fc2_local[0]),
            spread_pick(own_pick, fc2_local[1]),
        ),
        ("dp", "row", "col"),
    )
    fc1_down_grad = take_block(summed_all[0], 1, row_index, fc1_down.shape[1])
    fc1_up_grad = take_block(summed_all[1], 2, col_index, fc1_up.shape[2])
    fc2_down_grad = take_block(summed_all[2], 1, col_index, fc2_down.shape[1])
    fc2_up_grad = take_block(summed_all[3], 2, row_index, fc2_up.shape[2])
    result = ((middle + mlp_out) * validity).astype(jnp.bfloat16).T
    grad_branch = grad_middle.astype(jnp.bfloat16)
    grad_branch_rows = token_rows(grad_branch)
    grad_attended = head_cols(
        adapted_back(grad_branch_rows, proj_full, proj_dn, proj_upm).astype(jnp.bfloat16)
    )
    grad_qkv = attend_back(qkv_low, log_total, grad_attended, tables)
    grad_qkv_rows = token_rows(grad_qkv)
    grad_hidden_one = head_sums(adapted_back(grad_qkv_rows, qkv_full, qkv_dn, qkv_upm))
    qkv_pair = pair_grads(hidden_rows, grad_qkv_rows, qkv_dn, qkv_upm)
    proj_pair = pair_grads(attended_rows, grad_branch_rows, proj_dn, proj_upm)
    attn_sums = lax.psum(
        (
            spread_pick(own_pick, qkv_pair[0]),
            spread_pick(own_pick, qkv_pair[1]),
            spread_pick(own_pick, proj_pair[0]),
            spread_pick(own_pick, proj_pair[1]),
        ),
        ("dp", "row", "col"),
    )
    qkv_down_grad = take_block(attn_sums[0], 1, row_index, qkv_down.shape[1])
    qkv_up_grad = take_block(attn_sums[1], 2, col_index, qkv_up.shape[2])
    proj_down_grad = take_block(attn_sums[2], 1, col_index, proj_down.shape[1])
    proj_up_grad = take_block(attn_sums[3], 2, row_index, proj_up.shape[2])
    grad_inputs = (
        grad_middle + norm_backward(grad_hidden_one * validity * gain_one, normed_one, inv_one)
    ).T
    return (
        result,
        grad_inputs,
        qkv_down_grad,
        qkv_up_grad,
        proj_down_grad,
        proj_up_grad,
        fc1_down_grad,
        fc1_up_grad,
        fc2_down_grad,
        fc2_up_grad,
    )


def solution(mesh):
    return jax.shard_map(
        body,
        mesh=mesh,
        in_specs=(
            P("row", ("dp", "col")),
            P("row", ("dp", "col")),
            P(),
            P("row"),
            P("row"),
            P("row", "col"),
            P("col", "row"),
            P("row", "col"),
            P("row", "col"),
            P(),
            P(),
            P(None, "row", None),
            P(None, None, "col"),
            P(None, "col", None),
            P(None, None, "row"),
            P(None, "row", None),
            P(None, None, "col"),
            P(None, "col", None),
            P(None, None, "row"),
        ),
        out_specs=(
            P("row", ("dp", "col")),
            P("row", ("dp", "col")),
            P(None, "row", None),
            P(None, None, "col"),
            P(None, "col", None),
            P(None, None, "row"),
            P(None, "row", None),
            P(None, None, "col"),
            P(None, "col", None),
            P(None, None, "row"),
        ),
        check_vma=False,
    )
```

profile of v0, /device:TPU:0, one launch (start us, length us, event | category | flops | bytes accessed | tf_op | source)
XLA Modules:
  0.0 1826.9 jit_solution(15166732212104624496)
XLA Ops:
  46.7 118.0 %all_gather.54 = bf16[8,16,2304]{1,0,2:T(8,128)(2,1)} all-gather(bf16[8,16,576]{1,0,2:T(8,128)(2,1)S(1)} %copy.225), channel_id=1, replica_groups=mesh['dp'=2,'row'=4,'col'=4] {'col'}, dimensions={2}, use_global_device_ids=true | all-gather | bytes 737280 | tf_op jit(solution)/shard_map/all_gather | solution.py:252
  171.6 12.9 all_gather.62
  184.5 30.9 %all_gather.57 = bf16[8,768,16]{2,0,1:T(8,128)(2,1)S(1)} all-gather(bf16[8,192,16]{2,0,1:T(8,128)(2,1)} %copy.243), channel_id=1, replica_groups=mesh['dp'=2,'row'=4,'col'=4] {'col'}, dimensions={1}, use_global_device_ids=true | all-gather | bytes 245760 | tf_op jit(solution)/shard_map/all_gather | solution.py:253
  215.4 12.6 all_gather.53
  263.0 74.5 %all_gather.55 = bf16[192,768]{0,1:T(8,128)(2,1)S(1)} all-gather(bf16[192,192]{0,1:T(8,128)(2,1)S(1)} %copy.241), channel_id=1, replica_groups=mesh['dp'=2,'row'=4,'col'=4] {'row'}, dimensions={1}, use_global_device_ids=true | all-gather | bytes 368640 | tf_op jit(solution)/shard_map/all_gather | solution.py:245
  338.7 13.0 all_gather.58
  372.0 26.8 %reshape.211 = bf16[25,196,3,3,64]{1,0,4,3,2:T(8,128)(2,1)} reshape(bf16[4,1225,576]{1,0,2:T(4,128)(2,1)} %copy.227) | data formatting | bytes 11289600 | tf_op jit(solution)/shard_map/reshape | solution.py:142
  427.1 21.4 %add.271 = f32[25,3,14,14,14,14]{0,5,4,3,2,1:T(8,128)} broadcast(f32[25,3,14,14,14]{0,4,3,2,1:T(8,128)S(1)} %copy.236), dimensions={0,1,2,3,5} | broadcast | bytes 12348000 | tf_op jit(solution)/shard_map/add | solution.py:160
  448.6 64.5 %add.272 = f32[25,3,196,196]{0,3,2,1:T(8,128)} reshape(f32[25,3,14,14,14,14]{0,5,4,3,2,1:T(8,128)} %add.271) | data formatting | bytes 23049600 | tf_op jit(solution)/shard_map/add | solution.py:160
  513.1 39.1 %copy.237 = f32[25,3,196,196]{2,3,1,0:T(8,128)} copy(f32[25,3,196,196]{0,3,2,1:T(8,128)} %add.272) | data formatting | bytes 23049600 | tf_op jit(solution)/shard_map/add | solution.py:160
  563.4 22.8 %add.268 = f32[25,3,14,14,14,14]{0,5,4,3,2,1:T(8,128)} broadcast(f32[25,3,14,14,14]{0,4,3,2,1:T(8,128)} %copy.233), dimensions={0,1,2,3,4} | broadcast | bytes 12348000 | tf_op jit(solution)/shard_map/add | solution.py:160
  586.3 64.5 %add.269 = f32[25,3,196,196]{0,3,2,1:T(8,128)} reshape(f32[25,3,14,14,14,14]{0,5,4,3,2,1:T(8,128)} %add.268) | data formatting | bytes 23049600 | tf_op jit(solution)/shard_map/add | solution.py:160
  650.8 39.1 %copy.234 = f32[25,3,196,196]{2,3,1,0:T(8,128)} copy(f32[25,3,196,196]{0,3,2,1:T(8,128)} %add.269) | data formatting | bytes 23049600 | tf_op jit(solution)/shard_map/add | solution.py:160
  689.9 24.5 %fusion.132 = (f32[25,3,196]{2,1,0:T(4,128)S(1)}, f32[25,3,196,196]{2,3,1,0:T(8,128)}) fusion(f32[25,3,196,196]{2,3,1,0:T(8,128)} %copy.237, f32[25,3,196,196]{2,3,1,0:T(8,128)} %copy.234, bf16[25,196,3,1,64]{1,0,4,3,2:T(8,128)(2,1)} %get-tuple-element.37, bf16[25,196,3,1,64]{1,0,4,3,2:T(8,128)(2,1)S(1)} %copy-done.9), kind=kOutput, calls=%fused_computation.234 | convolution fusion | flops 380303744 | bytes 38396400 | tf_op jit(solution)/shard_map/nqhc,nkhc->nhqk/dot_general | solution.py:149
  779.3 33.6 %all_gather.67 = bf16[8,16,768]{1,0,2:T(8,128)(2,1)S(1)} all-gather(bf16[8,16,192]{1,0,2:T(8,128)(2,1)} %copy.250), channel_id=1, replica_groups=mesh['dp'=2,'row'=4,'col'=4] {'row'}, dimensions={2}, use_global_device_ids=true | all-gather | bytes 245760 | tf_op jit(solution)/shard_map/all_gather | solution.py:271
  814.5 19.3 %all_gather.66 = bf16[8,3072,16]{1,2,0:T(8,128)(2,1)S(1)} all-gather(bf16[8,768,16]{1,2,0:T(8,128)(2,1)} %param.36), channel_id=1, replica_groups=mesh['dp'=2,'row'=4,'col'=4] {'col'}, dimensions={1}, use_global_device_ids=true | all-gather | bytes 983040 | tf_op jit(solution)/shard_map/all_gather | solution.py:278
  868.1 30.2 %all_gather.63 = bf16[8,16,3072]{2,1,0:T(8,128)(2,1)S(1)} all-gather(bf16[8,16,768]{2,1,0:T(8,128)(2,1)S(1)} %copy-done.72), channel_id=1, replica_groups=mesh['dp'=2,'row'=4,'col'=4] {'col'}, dimensions={2}, use_global_device_ids=true | all-gather | bytes 983040 | tf_op jit(solution)/shard_map/all_gather | solution.py:277
  928.8 11.8 fusion.137
  940.6 12.5 all-to-all-done.4
  975.9 41.4 %multiply_convert_fusion.1 = (bf16[1225,3072]{1,0:T(8,128)(2,1)}, f32[1225,3072]{1,0:T(8,128)}, f32[1225,3072]{1,0:T(8,128)}) fusion(f32[1225,3072]{1,0:T(8,128)S(1)} %fusion.135, f32[1225,16]{0,1:T(8,128)S(1)} %fusion.149, bf16[1,16,3072]{2,0,1:T(2,128)(2,1)S(1)} %fusion.64), kind=kOutput, calls=%fused_computation.9 | convolution fusion | flops 970905600 | bytes 52861504 | tf_op jit(solution)/shard_map/dot_general | solution.py:110
  1017.3 23.1 %add_convert_fusion = bf16[1225,3072]{1,0:T(8,128)(2,1)} fusion(f32[1225,3072]{1,0:T(8,128)} %get-tuple-element.32, f32[1225,3072]{1,0:T(8,128)} %fusion.137, f32[1225,3072]{1,0:T(8,128)} %get-tuple-element.51, f32[1225,16]{0,1:T(8,128)S(1)} %fusion.116, bf16[1,3072,16]{1,2,0:T(8,128)(2,1)S(1)} %copy.292), kind=kOutput, calls=%fused_computation.8 | convolution fusion | flops 778982400 | bytes 52861504 | tf_op jit(solution)/shard_map/dot_general | solution.py:117
  1062.8 26.9 %all_to_all.186 = bf16[1225,4,192]{0,2,1:T(8,128)(2,1)S(1)} all-to-all(bf16[1225,4,192]{0,2,1:T(8,128)(2,1)S(1)} %bitcast.307), channel_id=1, replica_groups=mesh['dp'=2,'row'=4,'col'=4] {'row'}, dimensions={1} | all-to-all | bytes 3763200 | tf_op jit(solution)/shard_map/all_to_all | solution.py:88
  1114.9 23.5 %all-to-all-done.8 = bf16[4,1225,192]{1,2,0:T(8,128)(2,1)S(1)} async-done(((bf16[4,1225,192]{1,2,0:T(8,128)(2,1)}), bf16[4,1225,192]{1,2,0:T(8,128)(2,1)S(1)}, u32[]{:S(2)}, u32[]{:S(2)}) %all-to-all-start.8) | async-done | bytes 1881632 | tf_op jit(solution)/shard_map/all_to_all | solution.py:94
  1208.2 21.7 %multiply_reduce_fusion = (f32[25,3,196]{2,1,0:T(4,128)S(1)}, f32[25,3,196,196]{2,3,1,0:T(8,128)}) fusion(f32[25,3,196,196]{2,3,1,0:T(8,128)} %get-tuple-element.50, f32[25,3,196]{2,1,0:T(4,128)S(1)} %log_add_fusion, bf16[25,196,3,1,64]{1,0,4,3,2:T(8,128)(2,1)} %get-tuple-element.35, bf16[25,196,3,64]{1,0,3,2:T(8,128)(2,1)S(1)} %reshape.212), kind=kOutput, calls=%fused_computation.2 | convolution fusion | flops 377422528 | bytes 26930400 | tf_op jit(solution)/shard_map/nqhc,nkhc->nhqk/dot_general | solution.py:185
  1249.0 30.3 %copy.261 = f32[25,3,196,196]{0,3,2,1:T(8,128)} copy(bf16[25,3,196,196]{2,3,1,0:T(8,128)(2,1)} %copy-done.2) | data formatting | bytes 17287200 | tf_op jit(solution)/shard_map/reshape | solution.py:194
  1279.4 64.6 %reshape.221 = f32[25,3,14,14,14,14]{0,5,4,3,2,1:T(8,128)} reshape(f32[25,3,196,196]{0,3,2,1:T(8,128)} %copy.261) | data formatting | bytes 23049600 | tf_op jit(solution)/shard_map/reshape | solution.py:194
  1344.0 94.7 %fusion.128 = (f32[25,3,14,14,14]{0,4,3,2,1:T(8,128)}, f32[25,3,14,14,14]{0,4,3,2,1:T(8,128)}) fusion(f32[25,3,14,14,14,14]{0,5,4,3,2,1:T(8,128)} %reshape.221), kind=kLoop, calls=%fused_computation.231 | loop fusion | flops 5350800 | bytes 13171200 | tf_op jit(solution)/shard_map/reduce_sum | solution.py:195
  1494.7 11.8 copy.269
  1506.5 24.2 %convert_element_type.249 = bf16[4,1225,576]{1,0,2:T(4,128)(2,1)} reshape(bf16[25,196,3,3,64]{1,0,4,3,2:T(8,128)(2,1)} %copy.269) | data formatting | bytes 11289600 | tf_op jit(solution)/shard_map/convert_element_type | solution.py:205
  1577.8 31.0 %all-to-all-done.10 = bf16[4,1225,576]{1,2,0:T(8,128)(2,1)} async-done(((bf16[4,1225,576]{1,2,0:T(8,128)(2,1)}), bf16[4,1225,576]{1,2,0:T(8,128)(2,1)}, u32[]{:S(2)}, u32[]{:S(2)}) %all-to-all-start.10) | async-done | bytes 5644832 | tf_op jit(solution)/shard_map/all_to_all | solution.py:94
  1643.2 17.6 all-to-all-done.11
  1699.4 106.6 %all-reduce.6.cloned.1.call-done = (f32[8,768,16]{1,2,0:T(8,128)}, f32[8,16,2304]{2,1,0:T(8,128)}, f32[8,768,16]{1,2,0:T(8,128)}, f32[8,16,768]{2,1,0:T(8,128)},...) async-done(((f32[8,768,16]{1,2,0:T(8,128)}, f32[8,16,2304]{2,1,0:T(8,128)}, f32[8,768,16]{1,2,0:T(8,128)}, ...) | async-done | bytes 6291472 | tf_op jit(solution)/shard_map/psum | solution.py:326
  (386 shorter events, 621.0 us)
Async XLA Ops:
  7.2 354.6 %copy-start = (bf16[27,64]{1,0:T(8,128)(2,1)S(1)}, bf16[27,64]{1,0:T(8,128)(2,1)}, u32[]{:S(2)}) copy-start(bf16[27,64]{1,0:T(8,128)(2,1)} %param.28) | copy-start | bytes 10372
  7.2 225.9 %all-gather.7.cloned.1.call-start = ((), (), s32[]{:S(2)}) async-start(), calls=%async_computation.12 | async-start | bytes 4423680 | tf_op jit(solution)/shard_map/all_gather | solution.py:250
  41.5 191.2 %all-to-all-start = ((bf16[4,1225,192]{1,2,0:T(8,128)(2,1)}), bf16[4,1225,192]{1,2,0:T(8,128)(2,1)S(1)}, u32[]{:S(2)}, u32[]{:S(2)}) async-start(bf16[4,1225,192]{1,2,0:T(8,128)(2,1)} %copy.222), calls=%async_computation | async-start | bytes 3932160 | tf_op jit(solution)/shard_map/all_to_all | solution.py:94
  45.1 119.6 %copy-start.76 = (bf16[8,192,16]{1,2,0:T(8,128)(2,1)S(1)}, bf16[8,192,16]{1,2,0:T(8,128)(2,1)}, u32[]{:S(2)}) copy-start(bf16[8,192,16]{1,2,0:T(8,128)(2,1)} %param.34) | copy-start | bytes 147460
  45.1 317.2 %all-gather.15.cloned.1.call-start = ((), (), s32[]{:S(2)}) async-start(), calls=%async_computation.16 | async-start | bytes 1474560 | tf_op jit(solution)/shard_map/all_gather | solution.py:269
  45.9 119.1 %copy-start.77 = (bf16[8,192,16]{1,2,0:T(8,128)(2,1)S(1)}, bf16[8,192,16]{1,2,0:T(8,128)(2,1)}, u32[]{:S(2)}) copy-start(bf16[8,192,16]{1,2,0:T(8,128)(2,1)} %param.32) | copy-start | bytes 147460
  45.9 120.1 %copy-start.78 = (bf16[8,192,16]{1,2,0:T(8,128)(2,1)S(1)}, bf16[8,192,16]{1,2,0:T(8,128)(2,1)}, u32[]{:S(2)}) copy-start(bf16[8,192,16]{1,2,0:T(8,128)(2,1)} %param.30) | copy-start | bytes 147460
  171.6 56.4 %copy-start.91 = (s32[8,1]{0,1:T(1,128)S(1)}, s32[8,1]{0,1:T(1,128)}, u32[]{:S(2)}) copy-start(s32[8,1]{0,1:T(1,128)} %param.21) | copy-start | bytes 100
  256.5 81.9 %copy-start.79 = (bf16[8,16,192]{2,1,0:T(8,128)(2,1)S(1)}, bf16[8,16,192]{2,1,0:T(8,128)(2,1)}, u32[]{:S(2)}) copy-start(bf16[8,16,192]{2,1,0:T(8,128)(2,1)} %param.33) | copy-start | bytes 147460
  256.5 105.8 %all-to-all-start.1 = ((bf16[1225,4,576]{0,2,1:T(8,128)(2,1)}), bf16[1225,4,576]{0,2,1:T(8,128)(2,1)}, u32[]{:S(2)}, u32[]{:S(2)}) async-start(bf16[1225,4,576]{0,2,1:T(8,128)(2,1)} %bitcast.293), calls=%async_computation.1 | async-start | bytes 11796480 | tf_op jit(solution)/shard_map/all_to_all | solution.py:98
  261.8 91.5 %copy-start.93 = (u32[32]{0:T(128)S(1)}, u32[32]{0:T(128)}, u32[]{:S(2)}) copy-start(u32[32]{0:T(128)} %constant.173) | copy-start | bytes 388
  261.8 92.7 %copy-start.92 = (bf16[192]{0:T(256)(128)(2,1)S(1)}, bf16[192]{0:T(256)(128)(2,1)}, u32[]{:S(2)}) copy-start(bf16[192]{0:T(256)(128)(2,1)} %param.23) | copy-start | bytes 1156
  261.8 100.2 %copy-start.89 = (bf16[27,64]{1,0:T(8,128)(2,1)S(1)}, bf16[27,64]{1,0:T(8,128)(2,1)}, u32[]{:S(2)}) copy-start(bf16[27,64]{1,0:T(8,128)(2,1)} %param.29) | copy-start | bytes 10372
  261.9 572.0 %all-gather.11.cloned.1.call-start = ((), (), s32[]{:S(2)}) async-start(), calls=%async_computation.14 | async-start | bytes 1474560 | tf_op jit(solution)/shard_map/all_gather | solution.py:268
  262.6 571.3 %all-gather.9.cloned.1.call-start = ((), (), s32[]{:S(2)}) async-start(), calls=%async_computation.13 | async-start | bytes 1474560 | tf_op jit(solution)/shard_map/all_gather | solution.py:251
  338.4 590.4 %all-gather.17.cloned.1.call-start = ((), (), s32[]{:S(2)}) async-start(), calls=%async_computation.17 | async-start | bytes 5898240 | tf_op jit(solution)/shard_map/all_gather | solution.py:276
  362.0 190.1 %copy-start.63 = (bf16[14,14,64,1,1]{2,1,4,3,0:T(8,128)(2,1)}, bf16[14,14,64,1,1]{2,1,4,3,0:T(8,128)(2,1)S(1)}, u32[]{:S(2)}) copy-start(bf16[14,14,64,1,1]{2,1,4,3,0:T(8,128)(2,1)S(1)} %fusion.61) | copy-start | bytes 75268
  746.5 27.9 %all-to-all-start.2 = ((bf16[4,1225,192]{1,2,0:T(8,128)(2,1)}), bf16[4,1225,192]{1,2,0:T(8,128)(2,1)S(1)}, u32[]{:S(2)}, u32[]{:S(2)}) async-start(bf16[4,1225,192]{1,2,0:T(8,128)(2,1)} %copy.240), calls=%async_computation.2 | async-start | bytes 3932160 | tf_op jit(solution)/shard_map/all_to_all | solution.py:94
  775.7 70.0 %all-to-all-start.6 = ((bf16[4,1225,192]{1,2,0:T(8,128)(2,1)}), bf16[4,1225,192]{1,2,0:T(8,128)(2,1)S(1)}, u32[]{:S(2)}, u32[]{:S(2)}) async-start(bf16[4,1225,192]{1,2,0:T(8,128)(2,1)} %copy.253), calls=%async_computation.6 | async-start | bytes 3932160 | tf_op jit(solution)/shard_map/all_to_all | solution.py:82
  779.3 188.6 %all-gather.13.cloned.1.call-start = ((), (), s32[]{:S(2)}) async-start(), calls=%async_computation.15 | async-start | bytes 5898240 | tf_op jit(solution)/shard_map/all_gather | solution.py:275
  845.7 53.6 %all-to-all-start.3 = ((bf16[1225,4,192]{0,2,1:T(8,128)(2,1)}), bf16[1225,4,192]{0,2,1:T(8,128)(2,1)}, u32[]{:S(2)}, u32[]{:S(2)}) async-start(bf16[1225,4,192]{0,2,1:T(8,128)(2,1)} %bitcast.305), calls=%async_computation.3 | async-start | bytes 3932160 | tf_op jit(solution)/shard_map/all_to_all | solution.py:102
  867.8 149.5 %copy-start.55 = (bf16[1,3072,16]{1,2,0:T(8,128)(2,1)}, bf16[1,3072,16]{1,2,0:T(8,128)(2,1)S(1)}, u32[]{:S(2)}) copy-start(bf16[1,3072,16]{1,2,0:T(8,128)(2,1)S(1)} %copy.292) | copy-start | bytes 294916
  899.3 118.0 %copy-start.61 = (f32[1225,16]{0,1:T(8,128)}, f32[1225,16]{0,1:T(8,128)S(1)}, u32[]{:S(2)}) copy-start(f32[1225,16]{0,1:T(8,128)S(1)} %fusion.116) | copy-start | bytes 235204
  924.1 29.0 %all-to-all-start.4 = ((bf16[4,1225,192]{1,2,0:T(8,128)(2,1)}), bf16[4,1225,192]{1,2,0:T(8,128)(2,1)}, u32[]{:S(2)}, u32[]{:S(2)}) async-start(bf16[4,1225,192]{1,2,0:T(8,128)(2,1)} %copy.247), calls=%async_computation.4 | async-start | bytes 3932160 | tf_op jit(solution)/shard_map/all_to_all | solution.py:82
  1110.5 27.9 %all-to-all-start.8 = ((bf16[4,1225,192]{1,2,0:T(8,128)(2,1)}), bf16[4,1225,192]{1,2,0:T(8,128)(2,1)S(1)}, u32[]{:S(2)}, u32[]{:S(2)}) async-start(bf16[4,1225,192]{1,2,0:T(8,128)(2,1)} %copy.256), calls=%async_computation.8 | async-start | bytes 3932160 | tf_op jit(solution)/shard_map/all_to_all | solution.py:94
  1149.2 29.3 %all-to-all-start.9 = ((bf16[1225,4,192]{0,2,1:T(8,128)(2,1)}), bf16[1225,4,192]{0,2,1:T(8,128)(2,1)}, u32[]{:S(2)}, u32[]{:S(2)}) async-start(bf16[1225,4,192]{0,2,1:T(8,128)(2,1)} %bitcast.306), calls=%async_computation.9 | async-start | bytes 3932160 | tf_op jit(solution)/shard_map/all_to_all | solution.py:98
  1178.5 358.2 %all-to-all-start.5 = ((bf16[1225,4,192]{0,2,1:T(8,128)(2,1)}), bf16[1225,4,192]{0,2,1:T(8,128)(2,1)}, u32[]{:S(2)}, u32[]{:S(2)}) async-start(bf16[1225,4,192]{0,2,1:T(8,128)(2,1)} %bitcast.38), calls=%async_computation.5 | async-start | bytes 3932160 | tf_op jit(solution)/shard_map/all_to_all | solution.py:88
  1343.9 94.8 %copy-start.66 = (bf16[14,14,64]{2,1,0:T(8,128)(2,1)S(1)}, bf16[14,14,64]{2,1,0:T(8,128)(2,1)}, u32[]{:S(2)}) copy-start(bf16[14,14,64]{2,1,0:T(8,128)(2,1)} %copy-done.65) | copy-start | bytes 75268
  1536.7 72.1 %all-to-all-start.10 = ((bf16[4,1225,576]{1,2,0:T(8,128)(2,1)}), bf16[4,1225,576]{1,2,0:T(8,128)(2,1)}, u32[]{:S(2)}, u32[]{:S(2)}) async-start(bf16[4,1225,576]{1,2,0:T(8,128)(2,1)} %copy.270), calls=%async_computation.10 | async-start | bytes 11796480 | tf_op jit(solution)/shard_map/all_to_all | solution.py:94
  1627.2 33.6 %all-to-all-start.11 = ((bf16[1225,4,192]{0,2,1:T(8,128)(2,1)}), bf16[1225,4,192]{0,2,1:T(8,128)(2,1)}, u32[]{:S(2)}, u32[]{:S(2)}) async-start(bf16[1225,4,192]{0,2,1:T(8,128)(2,1)} %bitcast.304), calls=%async_computation.11 | async-start | bytes 3932160 | tf_op jit(solution)/shard_map/all_to_all | solution.py:102
  1631.8 174.2 %all-reduce.6.cloned.1.call-start = ((), (), s32[]{:S(2)}) async-start(), calls=%async_computation.18 | async-start | bytes 12582912 | tf_op jit(solution)/shard_map/psum | solution.py:326
  1689.6 130.2 %copy-start.1 = (bf16[27,64]{1,0:T(8,128)(2,1)S(1)}, bf16[27,64]{1,0:T(8,128)(2,1)}, u32[]{:S(2)}) copy-start(bf16[27,64]{1,0:T(8,128)(2,1)} %param.28) | copy-start | bytes 10372
  (84 other events, 808.3 us)
Sparse Core Ops, SparseCore 0:
  20.2 108.6 all-gather.6
  130.5 16.0 all-gather.14
  264.3 24.6 all-gather.10
  338.5 29.8 all-gather.8
  369.8 88.5 all-gather.16
  834.0 100.3 all-gather.12
  1643.3 162.6 all-reduce.5
where the time goes:
time: 1840 us; the launch traced here: 1830 us
  local copies, waits for them, and re-layouts  647 us (35%)
  blocking collectives  412 us (22%)
  matrix products  314 us (17%)
  waiting for transfers between devices  211 us (11%)
  other arithmetic  177 us (10%)
  starting transfers between devices  49.4 us (3%)
    add x6, local copies, waits for them, and re-layouts, score_matrix(): shaped + rel_rows[:, :, :, :, :, None] + rel_cols[:, :, :, :, None, :]  251 us
    all_gather x1, blocking collectives, body(): lax.all_gather(qkv_up, 'col', axis=2, tiled=True)  118 us
    psum x1, waiting for transfers between devices, body(): lax.psum((spread_pick(own_pick, qkv_pair[0]), spread_pick(own_pick, qkv_p...  107 us
    reshape x2, local copies, waits for them, and re-layouts, attend_back(): grad_s.astype(jnp.float32).reshape(windows, heads_local, WIN, WIN, WIN, WIN)  94.9 us
    reduce_sum x1, other arithmetic, attend_back(): along_rows = jnp.sum(split_grad, axis=5)  94.7 us
    all_gather x1, blocking collectives, body(): lax.all_gather(proj_weight, 'row', axis=1, tiled=True)  74.5 us
    all_to_all x4, waiting for transfers between devices, token_rows(): lax.all_to_all(values, 'row', split_axis=0, concat_axis=1, tiled=True)  65.1 us
    dot_general x4, matrix products, adapted_local(): jnp.dot(reduced, up_mat.astype(jnp.float32), precision=PRECISE)  53.4 us
  transfers between devices with their start and end apart: 18, of which 7 were waited for; matrix products, arithmetic and copies ran while one was open for 52% of the time, Pallas kernels for 0%

commit v1 on v0

--- a/solution.py
+++ b/solution.py
@@ -91,7 +91,10 @@
 
 
 def token_rows(values):
-    return lax.all_to_all(values, "row", split_axis=0, concat_axis=1, tiled=True)
+    return jnp.concatenate(
+        lax.all_to_all(jnp.stack(jnp.split(values, lax.axis_size("row"), axis=0)), "row", 0, 0),
+        axis=1,
+    )
 
 
 def head_cols(values):

time: 1840 us -> 1830 us (level)
  local copies, waits for them, and re-layouts: 647 us -> 623 us
where the time goes in v1:
time: 1830 us; the launch traced here: 1810 us
  local copies, waits for them, and re-layouts  623 us (34%)
  blocking collectives  418 us (23%)
  matrix products  314 us (17%)
  waiting for transfers between devices  211 us (12%)
  other arithmetic  182 us (10%)
  starting transfers between devices  49.3 us (3%)
    add x6, local copies, waits for them, and re-layouts, score_matrix(): shaped + rel_rows[:, :, :, :, :, None] + rel_cols[:, :, :, :, None, :]  252 us
    all_gather x1, blocking collectives, body(): lax.all_gather(qkv_up, 'col', axis=2, tiled=True)  123 us
    psum x1, waiting for transfers between devices, body(): lax.psum((spread_pick(own_pick, qkv_pair[0]), spread_pick(own_pick, qkv_p...  106 us
    reshape x2, local copies, waits for them, and re-layouts, attend_back(): grad_s.astype(jnp.float32).reshape(windows, heads_local, WIN, WIN, WIN, WIN)  95.1 us
    reduce_sum x1, other arithmetic, attend_back(): along_rows = jnp.sum(split_grad, axis=5)  94.7 us
    all_gather x1, blocking collectives, body(): lax.all_gather(proj_weight, 'row', axis=1, tiled=True)  74.5 us
    all_to_all x4, waiting for transfers between devices, token_rows(): lax.all_to_all(jnp.stack(jnp.split(values, lax.axis_size('row'), axis=0))...  65.1 us
    dot_general x4, matrix products, adapted_local(): jnp.dot(reduced, up_mat.astype(jnp.float32), precision=PRECISE)  53.5 us
  transfers between devices with their start and end apart: 18, of which 7 were waited for; matrix products, arithmetic and copies ran while one was open for 52% of the time, Pallas kernels for 0%

profile of v1, /device:TPU:0, one launch (start us, length us, event | category | flops | bytes accessed | tf_op | source)
XLA Modules:
  0.0 1813.3 jit_solution(8592601042739473367)
XLA Ops:
  41.2 123.5 %all_gather.54 = bf16[8,16,2304]{1,0,2:T(8,128)(2,1)} all-gather(bf16[8,16,576]{1,0,2:T(8,128)(2,1)S(1)} %copy.208), channel_id=1, replica_groups=mesh['dp'=2,'row'=4,'col'=4] {'col'}, dimensions={2}, use_global_device_ids=true | all-gather | bytes 737280 | tf_op jit(solution)/shard_map/all_gather | solution.py:255
  171.6 12.9 all_gather.62
  184.4 30.8 %all_gather.57 = bf16[8,768,16]{2,0,1:T(8,128)(2,1)S(1)} all-gather(bf16[8,192,16]{2,0,1:T(8,128)(2,1)} %copy.225), channel_id=1, replica_groups=mesh['dp'=2,'row'=4,'col'=4] {'col'}, dimensions={1}, use_global_device_ids=true | all-gather | bytes 245760 | tf_op jit(solution)/shard_map/all_gather | solution.py:256
  215.2 12.6 all_gather.53
  262.8 74.5 %all_gather.55 = bf16[192,768]{0,1:T(8,128)(2,1)S(1)} all-gather(bf16[192,192]{0,1:T(8,128)(2,1)S(1)} %copy.223), channel_id=1, replica_groups=mesh['dp'=2,'row'=4,'col'=4] {'row'}, dimensions={1}, use_global_device_ids=true | all-gather | bytes 368640 | tf_op jit(solution)/shard_map/all_gather | solution.py:248
  338.5 13.0 all_gather.58
  371.8 26.8 %reshape.223 = bf16[25,196,3,3,64]{1,0,4,3,2:T(8,128)(2,1)} reshape(bf16[4,1225,576]{1,0,2:T(4,128)(2,1)} %copy.210) | data formatting | bytes 11289600 | tf_op jit(solution)/shard_map/reshape | solution.py:145
  427.0 21.5 %add.271 = f32[25,3,14,14,14,14]{0,5,4,3,2,1:T(8,128)} broadcast(f32[25,3,14,14,14]{0,4,3,2,1:T(8,128)S(1)} %copy.219), dimensions={0,1,2,3,5} | broadcast | bytes 12348000 | tf_op jit(solution)/shard_map/add | solution.py:163
  448.5 64.5 %add.272 = f32[25,3,196,196]{0,3,2,1:T(8,128)} reshape(f32[25,3,14,14,14,14]{0,5,4,3,2,1:T(8,128)} %add.271) | data formatting | bytes 23049600 | tf_op jit(solution)/shard_map/add | solution.py:163
  513.0 39.1 %copy.220 = f32[25,3,196,196]{2,3,1,0:T(8,128)} copy(f32[25,3,196,196]{0,3,2,1:T(8,128)} %add.272) | data formatting | bytes 23049600 | tf_op jit(solution)/shard_map/add | solution.py:163
  563.4 22.8 %add.268 = f32[25,3,14,14,14,14]{0,5,4,3,2,1:T(8,128)} broadcast(f32[25,3,14,14,14]{0,4,3,2,1:T(8,128)} %copy.216), dimensions={0,1,2,3,4} | broadcast | bytes 12348000 | tf_op jit(solution)/shard_map/add | solution.py:163
  586.3 64.5 %add.269 = f32[25,3,196,196]{0,3,2,1:T(8,128)} reshape(f32[25,3,14,14,14,14]{0,5,4,3,2,1:T(8,128)} %add.268) | data formatting | bytes 23049600 | tf_op jit(solution)/shard_map/add | solution.py:163
  650.8 39.1 %copy.217 = f32[25,3,196,196]{2,3,1,0:T(8,128)} copy(f32[25,3,196,196]{0,3,2,1:T(8,128)} %add.269) | data formatting | bytes 23049600 | tf_op jit(solution)/shard_map/add | solution.py:163
  689.9 24.7 %fusion.132 = (f32[25,3,196]{2,1,0:T(4,128)S(1)}, f32[25,3,196,196]{2,3,1,0:T(8,128)}) fusion(f32[25,3,196,196]{2,3,1,0:T(8,128)} %copy.220, f32[25,3,196,196]{2,3,1,0:T(8,128)} %copy.217, bf16[25,196,3,1,64]{1,0,4,3,2:T(8,128)(2,1)} %get-tuple-element.37, bf16[25,196,3,1,64]{1,0,4,3,2:T(8,128)(2,1)S(1)} %copy-done.9), kind=kOutput, calls=%fused_computation.254 | convolution fusion | flops 380303744 | bytes 38396400 | tf_op jit(solution)/shard_map/nqhc,nkhc->nhqk/dot_general | solution.py:152
  777.1 33.6 %all_gather.67 = bf16[8,16,768]{1,0,2:T(8,128)(2,1)S(1)} all-gather(bf16[8,16,192]{1,0,2:T(8,128)(2,1)} %copy.232), channel_id=1, replica_groups=mesh['dp'=2,'row'=4,'col'=4] {'row'}, dimensions={2}, use_global_device_ids=true | all-gather | bytes 245760 | tf_op jit(solution)/shard_map/all_gather | solution.py:274
  812.3 19.4 %all_gather.66 = bf16[8,3072,16]{1,2,0:T(8,128)(2,1)S(1)} all-gather(bf16[8,768,16]{1,2,0:T(8,128)(2,1)} %param.36), channel_id=1, replica_groups=mesh['dp'=2,'row'=4,'col'=4] {'col'}, dimensions={1}, use_global_device_ids=true | all-gather | bytes 983040 | tf_op jit(solution)/shard_map/all_gather | solution.py:281
  865.8 30.4 %all_gather.63 = bf16[8,16,3072]{2,1,0:T(8,128)(2,1)S(1)} all-gather(bf16[8,16,768]{2,1,0:T(8,128)(2,1)S(1)} %copy-done.72), channel_id=1, replica_groups=mesh['dp'=2,'row'=4,'col'=4] {'col'}, dimensions={2}, use_global_device_ids=true | all-gather | bytes 983040 | tf_op jit(solution)/shard_map/all_gather | solution.py:280
  926.9 11.9 fusion.137
  938.7 12.4 all-to-all-done.4
  974.0 41.4 %multiply_convert_fusion.1 = (bf16[1225,3072]{1,0:T(8,128)(2,1)}, f32[1225,3072]{1,0:T(8,128)}, f32[1225,3072]{1,0:T(8,128)}) fusion(f32[1225,3072]{1,0:T(8,128)S(1)} %fusion.135, f32[1225,16]{0,1:T(8,128)S(1)} %fusion.149, bf16[1,16,3072]{2,0,1:T(2,128)(2,1)S(1)} %fusion.64), kind=kOutput, calls=%fused_computation.9 | convolution fusion | flops 970905600 | bytes 52861504 | tf_op jit(solution)/shard_map/dot_general | solution.py:113
  1015.5 22.8 %add_convert_fusion = bf16[1225,3072]{1,0:T(8,128)(2,1)} fusion(f32[1225,3072]{1,0:T(8,128)} %get-tuple-element.32, f32[1225,3072]{1,0:T(8,128)} %fusion.137, f32[1225,3072]{1,0:T(8,128)} %get-tuple-element.67, f32[1225,16]{0,1:T(8,128)S(1)} %fusion.116, bf16[1,3072,16]{1,2,0:T(8,128)(2,1)S(1)} %copy.272), kind=kOutput, calls=%fused_computation.8 | convolution fusion | flops 778982400 | bytes 52861504 | tf_op jit(solution)/shard_map/dot_general | solution.py:120
  1060.7 27.0 %all_to_all.136 = bf16[1225,4,192]{0,2,1:T(8,128)(2,1)S(1)} all-to-all(bf16[1225,4,192]{0,2,1:T(8,128)(2,1)S(1)} %bitcast.335), channel_id=1, replica_groups=mesh['dp'=2,'row'=4,'col'=4] {'row'}, dimensions={1} | all-to-all | bytes 3763200 | tf_op jit(solution)/shard_map/all_to_all | solution.py:88
  1107.4 23.5 %all-to-all-done.8 = bf16[4,1225,192]{1,2,0:T(8,128)(2,1)S(1)} async-done(((bf16[4,1225,192]{1,2,0:T(8,128)(2,1)}), bf16[4,1225,192]{1,2,0:T(8,128)(2,1)S(1)}, u32[]{:S(2)}, u32[]{:S(2)}) %all-to-all-start.8) | async-done | bytes 1881632 | tf_op jit(solution)/shard_map/all_to_all | solution.py:95
  1200.6 21.7 %multiply_reduce_fusion = (f32[25,3,196]{2,1,0:T(4,128)S(1)}, f32[25,3,196,196]{2,3,1,0:T(8,128)}) fusion(f32[25,3,196,196]{2,3,1,0:T(8,128)} %get-tuple-element.66, f32[25,3,196]{2,1,0:T(4,128)S(1)} %log_add_fusion, bf16[25,196,3,1,64]{1,0,4,3,2:T(8,128)(2,1)} %get-tuple-element.35, bf16[25,196,3,64]{1,0,3,2:T(8,128)(2,1)S(1)} %reshape.228), kind=kOutput, calls=%fused_computation.2 | convolution fusion | flops 377422528 | bytes 26930400 | tf_op jit(solution)/shard_map/nqhc,nkhc->nhqk/dot_general | solution.py:188
  1241.4 30.4 %copy.242 = f32[25,3,196,196]{0,3,2,1:T(8,128)} copy(bf16[25,3,196,196]{2,3,1,0:T(8,128)(2,1)} %copy-done.2) | data formatting | bytes 17287200 | tf_op jit(solution)/shard_map/reshape | solution.py:197
  1271.8 64.7 %reshape.239 = f32[25,3,14,14,14,14]{0,5,4,3,2,1:T(8,128)} reshape(f32[25,3,196,196]{0,3,2,1:T(8,128)} %copy.242) | data formatting | bytes 23049600 | tf_op jit(solution)/shard_map/reshape | solution.py:197
  1336.6 94.7 %fusion.128 = (f32[25,3,14,14,14]{0,4,3,2,1:T(8,128)}, f32[25,3,14,14,14]{0,4,3,2,1:T(8,128)}) fusion(f32[25,3,14,14,14,14]{0,5,4,3,2,1:T(8,128)} %reshape.239), kind=kLoop, calls=%fused_computation.251 | loop fusion | flops 5350800 | bytes 13171200 | tf_op jit(solution)/shard_map/reduce_sum | solution.py:198
  1487.3 11.8 copy.250
  1499.2 15.7 convert_element_type.247
  1564.3 31.1 %all-to-all-done.10 = bf16[4,1225,576]{1,2,0:T(8,128)(2,1)} async-done(((bf16[4,1225,576]{1,2,0:T(8,128)(2,1)}), bf16[4,1225,576]{1,2,0:T(8,128)(2,1)}, u32[]{:S(2)}, u32[]{:S(2)}) %all-to-all-start.10) | async-done | bytes 5644832 | tf_op jit(solution)/shard_map/all_to_all | solution.py:95
  1629.6 17.6 all-to-all-done.11
  1685.9 106.5 %all-reduce.6.cloned.1.call-done = (f32[8,768,16]{1,2,0:T(8,128)}, f32[8,16,2304]{2,1,0:T(8,128)}, f32[8,768,16]{1,2,0:T(8,128)}, f32[8,16,768]{2,1,0:T(8,128)},...) async-done(((f32[8,768,16]{1,2,0:T(8,128)}, f32[8,16,2304]{2,1,0:T(8,128)}, f32[8,768,16]{1,2,0:T(8,128)}, ...) | async-done | bytes 6291472 | tf_op jit(solution)/shard_map/psum | solution.py:329
  (388 shorter events, 609.8 us)
Async XLA Ops:
  7.2 354.4 %copy-start = (bf16[27,64]{1,0:T(8,128)(2,1)S(1)}, bf16[27,64]{1,0:T(8,128)(2,1)}, u32[]{:S(2)}) copy-start(bf16[27,64]{1,0:T(8,128)(2,1)} %param.28) | copy-start | bytes 10372
  7.2 225.6 %all-gather.7.cloned.1.call-start = ((), (), s32[]{:S(2)}) async-start(), calls=%async_computation.12 | async-start | bytes 4423680 | tf_op jit(solution)/shard_map/all_gather | solution.py:253
  36.0 196.5 %all-to-all-start = ((bf16[4,1225,192]{1,2,0:T(8,128)(2,1)}), bf16[4,1225,192]{1,2,0:T(8,128)(2,1)S(1)}, u32[]{:S(2)}, u32[]{:S(2)}) async-start(bf16[4,1225,192]{1,2,0:T(8,128)(2,1)} %pad_maximum_fusion.2), calls=%async_computation | async-start | bytes 3932160 | tf_op jit(solution)/shard_map/all_to_all | solution.py:95
  39.6 125.1 %copy-start.76 = (bf16[8,192,16]{1,2,0:T(8,128)(2,1)S(1)}, bf16[8,192,16]{1,2,0:T(8,128)(2,1)}, u32[]{:S(2)}) copy-start(bf16[8,192,16]{1,2,0:T(8,128)(2,1)} %param.34) | copy-start | bytes 147460
  39.6 322.5 %all-gather.15.cloned.1.call-start = ((), (), s32[]{:S(2)}) async-start(), calls=%async_computation.16 | async-start | bytes 1474560 | tf_op jit(solution)/shard_map/all_gather | solution.py:272
  40.3 124.6 %copy-start.77 = (bf16[8,192,16]{1,2,0:T(8,128)(2,1)S(1)}, bf16[8,192,16]{1,2,0:T(8,128)(2,1)}, u32[]{:S(2)}) copy-start(bf16[8,192,16]{1,2,0:T(8,128)(2,1)} %param.32) | copy-start | bytes 147460
  40.3 125.5 %copy-start.78 = (bf16[8,192,16]{1,2,0:T(8,128)(2,1)S(1)}, bf16[8,192,16]{1,2,0:T(8,128)(2,1)}, u32[]{:S(2)}) copy-start(bf16[8,192,16]{1,2,0:T(8,128)(2,1)} %param.30) | copy-start | bytes 147460
  171.5 56.3 %copy-start.91 = (s32[8,1]{0,1:T(1,128)S(1)}, s32[8,1]{0,1:T(1,128)}, u32[]{:S(2)}) copy-start(s32[8,1]{0,1:T(1,128)} %param.21) | copy-start | bytes 100
  256.3 81.9 %copy-start.79 = (bf16[8,16,192]{2,1,0:T(8,128)(2,1)S(1)}, bf16[8,16,192]{2,1,0:T(8,128)(2,1)}, u32[]{:S(2)}) copy-start(bf16[8,16,192]{2,1,0:T(8,128)(2,1)} %param.33) | copy-start | bytes 147460
  256.3 105.8 %all-to-all-start.1 = ((bf16[1225,4,576]{0,2,1:T(8,128)(2,1)}), bf16[1225,4,576]{0,2,1:T(8,128)(2,1)}, u32[]{:S(2)}, u32[]{:S(2)}) async-start(bf16[1225,4,576]{0,2,1:T(8,128)(2,1)} %bitcast.321), calls=%async_computation.1 | async-start | bytes 11796480 | tf_op jit(solution)/shard_map/all_to_all | solution.py:101
  261.6 91.5 %copy-start.93 = (u32[32]{0:T(128)S(1)}, u32[32]{0:T(128)}, u32[]{:S(2)}) copy-start(u32[32]{0:T(128)} %constant.173) | copy-start | bytes 388
  261.6 92.7 %copy-start.92 = (bf16[192]{0:T(256)(128)(2,1)S(1)}, bf16[192]{0:T(256)(128)(2,1)}, u32[]{:S(2)}) copy-start(bf16[192]{0:T(256)(128)(2,1)} %param.23) | copy-start | bytes 1156
  261.6 100.2 %copy-start.89 = (bf16[27,64]{1,0:T(8,128)(2,1)S(1)}, bf16[27,64]{1,0:T(8,128)(2,1)}, u32[]{:S(2)}) copy-start(bf16[27,64]{1,0:T(8,128)(2,1)} %param.29) | copy-start | bytes 10372
  261.7 570.1 %all-gather.11.cloned.1.call-start = ((), (), s32[]{:S(2)}) async-start(), calls=%async_computation.14 | async-start | bytes 1474560 | tf_op jit(solution)/shard_map/all_gather | solution.py:271
  262.4 569.4 %all-gather.9.cloned.1.call-start = ((), (), s32[]{:S(2)}) async-start(), calls=%async_computation.13 | async-start | bytes 1474560 | tf_op jit(solution)/shard_map/all_gather | solution.py:254
  338.2 588.7 %all-gather.17.cloned.1.call-start = ((), (), s32[]{:S(2)}) async-start(), calls=%async_computation.17 | async-start | bytes 5898240 | tf_op jit(solution)/shard_map/all_gather | solution.py:279
  361.8 190.3 %copy-start.63 = (bf16[14,14,64,1,1]{2,1,4,3,0:T(8,128)(2,1)}, bf16[14,14,64,1,1]{2,1,4,3,0:T(8,128)(2,1)S(1)}, u32[]{:S(2)}) copy-start(bf16[14,14,64,1,1]{2,1,4,3,0:T(8,128)(2,1)S(1)} %fusion.61) | copy-start | bytes 75268
  744.3 27.9 %all-to-all-start.2 = ((bf16[4,1225,192]{1,2,0:T(8,128)(2,1)}), bf16[4,1225,192]{1,2,0:T(8,128)(2,1)S(1)}, u32[]{:S(2)}, u32[]{:S(2)}) async-start(bf16[4,1225,192]{1,2,0:T(8,128)(2,1)} %pad_maximum_fusion.3), calls=%async_computation.2 | async-start | bytes 3932160 | tf_op jit(solution)/shard_map/all_to_all | solution.py:95
  773.5 70.1 %all-to-all-start.6 = ((bf16[4,1225,192]{1,2,0:T(8,128)(2,1)}), bf16[4,1225,192]{1,2,0:T(8,128)(2,1)S(1)}, u32[]{:S(2)}, u32[]{:S(2)}) async-start(bf16[4,1225,192]{1,2,0:T(8,128)(2,1)} %copy.235), calls=%async_computation.6 | async-start | bytes 3932160 | tf_op jit(solution)/shard_map/all_to_all | solution.py:82
  777.1 188.9 %all-gather.13.cloned.1.call-start = ((), (), s32[]{:S(2)}) async-start(), calls=%async_computation.15 | async-start | bytes 5898240 | tf_op jit(solution)/shard_map/all_gather | solution.py:278
  843.6 53.7 %all-to-all-start.3 = ((bf16[1225,4,192]{0,2,1:T(8,128)(2,1)}), bf16[1225,4,192]{0,2,1:T(8,128)(2,1)}, u32[]{:S(2)}, u32[]{:S(2)}) async-start(bf16[1225,4,192]{0,2,1:T(8,128)(2,1)} %bitcast.333), calls=%async_computation.3 | async-start | bytes 3932160 | tf_op jit(solution)/shard_map/all_to_all | solution.py:105
  865.6 149.9 %copy-start.55 = (bf16[1,3072,16]{1,2,0:T(8,128)(2,1)}, bf16[1,3072,16]{1,2,0:T(8,128)(2,1)S(1)}, u32[]{:S(2)}) copy-start(bf16[1,3072,16]{1,2,0:T(8,128)(2,1)S(1)} %copy.272) | copy-start | bytes 294916
  897.2 118.3 %copy-start.61 = (f32[1225,16]{0,1:T(8,128)}, f32[1225,16]{0,1:T(8,128)S(1)}, u32[]{:S(2)}) copy-start(f32[1225,16]{0,1:T(8,128)S(1)} %fusion.116) | copy-start | bytes 235204
  922.0 29.2 %all-to-all-start.4 = ((bf16[4,1225,192]{1,2,0:T(8,128)(2,1)}), bf16[4,1225,192]{1,2,0:T(8,128)(2,1)}, u32[]{:S(2)}, u32[]{:S(2)}) async-start(bf16[4,1225,192]{1,2,0:T(8,128)(2,1)} %copy.229), calls=%async_computation.4 | async-start | bytes 3932160 | tf_op jit(solution)/shard_map/all_to_all | solution.py:82
  1103.0 27.9 %all-to-all-start.8 = ((bf16[4,1225,192]{1,2,0:T(8,128)(2,1)}), bf16[4,1225,192]{1,2,0:T(8,128)(2,1)S(1)}, u32[]{:S(2)}, u32[]{:S(2)}) async-start(bf16[4,1225,192]{1,2,0:T(8,128)(2,1)} %pad_maximum_fusion.4), calls=%async_computation.8 | async-start | bytes 3932160 | tf_op jit(solution)/shard_map/all_to_all | solution.py:95
  1141.6 29.4 %all-to-all-start.9 = ((bf16[1225,4,192]{0,2,1:T(8,128)(2,1)}), bf16[1225,4,192]{0,2,1:T(8,128)(2,1)}, u32[]{:S(2)}, u32[]{:S(2)}) async-start(bf16[1225,4,192]{0,2,1:T(8,128)(2,1)} %bitcast.334), calls=%async_computation.9 | async-start | bytes 3932160 | tf_op jit(solution)/shard_map/all_to_all | solution.py:101
  1171.1 352.2 %all-to-all-start.5 = ((bf16[1225,4,192]{0,2,1:T(8,128)(2,1)}), bf16[1225,4,192]{0,2,1:T(8,128)(2,1)}, u32[]{:S(2)}, u32[]{:S(2)}) async-start(bf16[1225,4,192]{0,2,1:T(8,128)(2,1)} %bitcast.46), calls=%async_computation.5 | async-start | bytes 3932160 | tf_op jit(solution)/shard_map/all_to_all | solution.py:88
  1336.6 94.8 %copy-start.66 = (bf16[14,14,64]{2,1,0:T(8,128)(2,1)S(1)}, bf16[14,14,64]{2,1,0:T(8,128)(2,1)}, u32[]{:S(2)}) copy-start(bf16[14,14,64]{2,1,0:T(8,128)(2,1)} %copy-done.65) | copy-start | bytes 75268
  1523.3 72.1 %all-to-all-start.10 = ((bf16[4,1225,576]{1,2,0:T(8,128)(2,1)}), bf16[4,1225,576]{1,2,0:T(8,128)(2,1)}, u32[]{:S(2)}, u32[]{:S(2)}) async-start(bf16[4,1225,576]{1,2,0:T(8,128)(2,1)} %pad_maximum_fusion.1), calls=%async_computation.10 | async-start | bytes 11796480 | tf_op jit(solution)/shard_map/all_to_all | solution.py:95
  1613.6 33.6 %all-to-all-start.11 = ((bf16[1225,4,192]{0,2,1:T(8,128)(2,1)}), bf16[1225,4,192]{0,2,1:T(8,128)(2,1)}, u32[]{:S(2)}, u32[]{:S(2)}) async-start(bf16[1225,4,192]{0,2,1:T(8,128)(2,1)} %bitcast.332), calls=%async_computation.11 | async-start | bytes 3932160 | tf_op jit(solution)/shard_map/all_to_all | solution.py:105
  1618.2 174.2 %all-reduce.6.cloned.1.call-start = ((), (), s32[]{:S(2)}) async-start(), calls=%async_computation.18 | async-start | bytes 12582912 | tf_op jit(solution)/shard_map/psum | solution.py:329
  1676.1 130.1 %copy-start.1 = (bf16[27,64]{1,0:T(8,128)(2,1)S(1)}, bf16[27,64]{1,0:T(8,128)(2,1)}, u32[]{:S(2)}) copy-start(bf16[27,64]{1,0:T(8,128)(2,1)} %param.28) | copy-start | bytes 10372
  (84 other events, 806.2 us)
Sparse Core Ops, SparseCore 0:
  20.1 114.6 all-gather.6
  136.4 15.3 all-gather.14
  264.1 24.7 all-gather.10
  338.3 29.9 all-gather.8
  369.7 88.5 all-gather.16
  831.9 100.3 all-gather.12
  1629.7 162.6 all-reduce.5
